TPU v7x, 32 devices: a whole 2x2x4 slice. The times are simulated.
32 devices in a mesh: dist: 4 (over y, x), rows: 8 (over z, core).
Axes of the slice: x: 2, y: 2, z: 4, core: 2. Of those that a mesh axis runs over, the one named last changes fastest.
Arguments:
- volume: bfloat16 [128, 128, 2048], P('rows', None, 'dist'), may hold values from -6 to 6
- kernels: bfloat16 [128, 2, 128, 128], P('rows'), may hold values from -0.09375 to 0.09375
- targets: int32 [128, 2], P('rows'), may hold values from 0 to 7, all different within a row; in each aligned block of 16 rows (0 to 15, 16 to 31, ...) at most 8 rows name the same one
- contrast: bfloat16 [4, 8, 128, 2048], P('dist', 'rows'), may hold values from -6 to 6
- fresnel_numbers: float32 [4], P('dist'), may hold values from 0.4 to 1.6
Outputs:
- gradient: bfloat16 [128, 128, 2048], P('rows', None, 'dist')
Inputs may be any that keep to these rules, and one draw needn't show every extreme that they name: `targets`: each row names 2 different detector blocks; among the rows of one index of rows no detector block is named more than 8 times, and some block is named exactly 8 times.
All inputs are finite; a program needn't handle non-finite values.
Results may differ from a plain program's by a relative error of at most 0.0063.
Values may be sent and summed in bfloat16 or wider, within the bound.
No kernel may reach another device: no remote copies, remote signals or barrier semaphores. Data moves between devices by JAX's collectives and lax.ppermute only.
A program may use at most 128 MiB of HBM per device.

v0:
```python
import math
import jax
import jax.numpy as jnp
from jax import lax
from jax.sharding import PartitionSpec as P


def spectral_table(width):
    half = width // 2
    index_rows = lax.broadcasted_iota(jnp.int32, (width, half), 0)
    index_cols = lax.broadcasted_iota(jnp.int32, (width, half), 1) + 1
    turns = (index_rows * index_cols % width).astype(jnp.float32) * (2.0 * math.pi / width)
    return jnp.concatenate([jnp.cos(turns), jnp.sin(turns)], axis=1)


def spectral_weight(width, number):
    half = width // 2
    freq = (lax.iota(jnp.int32, half) + 1).astype(jnp.float32)
    factor = jnp.sin(jnp.pi * number * freq * freq / width)
    scaled = factor * jnp.where(freq < half, 2.0, 1.0) / width
    return jnp.concatenate([scaled, scaled])


def shards(volume, kernels, targets, contrast, fresnel_numbers):
    owners = lax.axis_size("rows")
    vblocks, blk, quarter = volume.shape
    top = kernels.shape[1]
    items = vblocks * top
    width = contrast.shape[-1]
    contrib = jnp.einsum("btij,bjw->btiw", kernels, volume, preferred_element_type=jnp.float32)
    contrib = contrib.astype(jnp.bfloat16).reshape(items, blk * quarter)
    flat = targets.reshape(items)
    capacity = max(2, 2 * items // owners)
    later = lax.broadcasted_iota(jnp.int32, (items, items), 0)
    before = lax.broadcasted_iota(jnp.int32, (items, items), 1)
    same = (flat[:, None] == flat[None, :]) & (before < later)
    rank = jnp.sum(same.astype(jnp.int32), axis=1)
    slot = flat * capacity + rank
    place = (
        slot[None, :] == lax.broadcasted_iota(jnp.int32, (owners * capacity, items), 0)
    ).astype(jnp.bfloat16)
    outgoing = jnp.dot(place, contrib, preferred_element_type=jnp.float32).astype(jnp.bfloat16)
    outgoing = outgoing.reshape(owners, capacity, blk, quarter)
    arrived = lax.all_to_all(outgoing, "rows", split_axis=0, concat_axis=0, tiled=True)
    per_owner = jnp.sum(arrived.astype(jnp.float32), axis=1).astype(jnp.bfloat16)
    projection = jnp.sum(per_owner.astype(jnp.float32), axis=0)
    table = spectral_table(width)
    weight = spectral_weight(width, fresnel_numbers[0])
    spectrum = jnp.dot(
        lax.all_gather(projection, "dist", axis=1, tiled=True),
        table,
        precision=lax.Precision.HIGHEST,
        preferred_element_type=jnp.float32,
    )

    def synthesize(coeffs):
        return lax.dot_general(
            coeffs * weight,
            table,
            (((1,), (1,)), ((), ())),
            precision=lax.Precision.HIGHEST,
            preferred_element_type=jnp.float32,
        )

    residual = -2.0 * synthesize(spectrum) - contrast[0, 0].astype(jnp.float32)
    analysed = jnp.dot(
        residual, table, precision=lax.Precision.HIGHEST, preferred_element_type=jnp.float32
    )
    term = -2.0 * synthesize(analysed)
    summed = lax.psum(term, "dist")
    own_cols = lax.dynamic_slice_in_dim(summed, lax.axis_index("dist") * quarter, quarter, 1)
    image_gradient = own_cols.astype(jnp.bfloat16)
    piece = lax.all_gather(image_gradient[None], "rows", axis=0, tiled=True)
    count = piece.shape[0]
    pick = (flat[:, None] == lax.broadcasted_iota(jnp.int32, (items, count), 1)).astype(
        jnp.bfloat16
    )
    gathered = jnp.dot(
        pick, piece.reshape(count, blk * quarter), preferred_element_type=jnp.float32
    )
    chosen = gathered.astype(jnp.bfloat16).reshape(vblocks, top, blk, quarter)
    grad = jnp.einsum("btij,btiw->bjw", kernels, chosen, preferred_element_type=jnp.float32)
    return grad.astype(jnp.bfloat16)


def solution(mesh):
    in_specs = (
        P("rows", None, "dist"),
        P("rows", None, None, None),
        P("rows", None),
        P("dist", "rows", None, None),
        P("dist"),
    )
    out_specs = P("rows", None, "dist")
    return jax.shard_map(shards, mesh=mesh, in_specs=in_specs, out_specs=out_specs, check_vma=False)
```

profile of v0, /device:TPU:0, one launch (start us, length us, event | category | flops | bytes accessed | tf_op | source)
XLA Modules:
  0.0 398.6 jit_solution(16857438083517022711)
XLA Ops:
  6.5 0.9 copy.12
  7.4 0.1 eq.33
  7.5 0.2 convert_reduce_fusion.1
  7.7 0.4 copy-done
  8.1 2.5 convolution_convert_fusion.2
  10.6 2.4 copy.18
  13.0 2.3 convolution_convert_fusion
  15.3 190.8 %all_to_all.5 = bf16[8,8,128,512]{3,1,2,0:T(8,128)(2,1)} all-to-all(bf16[8,8,128,512]{3,1,2,0:T(8,128)(2,1)S(1)} %bitcast.32), channel_id=1, replica_groups=mesh['dist'=4,'rows'=8] {'rows'}, dimensions={0} | all-to-all | bytes 16777216 | tf_op jit(solution)/shard_map/all_to_all | solution.py:44
  206.1 9.2 %reduce_sum.31 = bf16[8,128,512]{2,1,0:T(8,128)(2,1)S(1)} reduce(bf16[8,8,128,512]{3,1,2,0:T(8,128)(2,1)} %all_to_all.5, bf16[]{:T(256)} %constant.18.clone.1), dimensions={1}, to_apply=%region_1.0 | reduce | flops 3670016 | bytes 9437186 | tf_op jit(solution)/shard_map/reduce_sum | solution.py:45
  215.3 0.8 convert_reduce_fusion
  216.2 0.6 all-gather.6.cloned.1.call-start
  217.5 34.4 %fusion.11 = (f32[2048,1024]{1,0:T(8,128)}, f32[2048,1024]{1,0:T(8,128)}) fusion(s32[1024]{0:T(1024)S(1)} %iota_add_fusion), kind=kLoop, calls=%fused_computation.18 | loop fusion | flops 29360128 | bytes 16781312 | tf_op jit(solution)/shard_map/cos | solution.py:13
  252.0 15.1 %fusion.12 = f32[128,2048]{1,0:T(8,128)S(1)} fusion(f32[128,2048]{1,0:T(8,128)} %all-gather.4.cloned.1.call-done, f32[2048,1024]{1,0:T(8,128)} %get-tuple-element.6, f32[2048,1024]{1,0:T(8,128)} %get-tuple-element.5, f32[2048]{0:T(1024)S(1)} %pad_maximum_fusion.15), kind=kOutput, calls=%fused_computation.20 | convolution fusion | flops 6446907392 | bytes 18882560 | tf_op jit(solution)/shard_map/dot_general | solution.py:49
  267.1 19.9 %fusion.16 = f32[128,2048]{1,0:T(8,128)S(1)} fusion(f32[128,2048]{1,0:T(8,128)S(1)} %fusion.12, f32[2048,1024]{1,0:T(8,128)} %get-tuple-element.6, f32[2048,1024]{1,0:T(8,128)S(1)} %copy-done.2, bf16[1,1,128,2048]{3,2,1,0:T(8,128)(2,1)S(1)} %copy-done.4), kind=kOutput, calls=%fused_computation.24 | convolution fusion | flops 6447431680 | bytes 19398656 | tf_op jit(solution)/shard_map/dot_general | solution.py:57
  287.0 11.0 %fusion.14 = f32[128,2048]{1,0:T(8,128)S(1)} fusion(f32[128,2048]{1,0:T(8,128)S(1)} %fusion.16, f32[2048,1024]{1,0:T(8,128)} %get-tuple-element.6, f32[2048,1024]{1,0:T(8,128)S(1)} %copy-done.2, f32[2048]{0:T(1024)S(1)} %pad_maximum_fusion.15), kind=kOutput, calls=%fused_computation.22 | convolution fusion | flops 6446907392 | bytes 18882560 | tf_op jit(solution)/shard_map/dot_general | solution.py:66
  297.9 19.9 %fusion.15 = f32[128,2048]{1,0:T(8,128)S(1)} fusion(f32[128,2048]{1,0:T(8,128)S(1)} %fusion.14, f32[2048,1024]{1,0:T(8,128)} %get-tuple-element.6, f32[2048,1024]{1,0:T(8,128)S(1)} %copy-done.2), kind=kOutput, calls=%fused_computation.23 | convolution fusion | flops 6446907392 | bytes 18874368 | tf_op jit(solution)/shard_map/dot_general | solution.py:57
  317.8 41.1 %all-reduce.1 = bf16[128,2048]{1,0:T(8,128)(2,1)S(1)} all-reduce(f32[128,2048]{1,0:T(8,128)S(1)} %fusion.15), channel_id=1, replica_groups=mesh['dist'=4,'rows'=8] {'dist'}, use_global_device_ids=true, to_apply=%region_3.4 | all-reduce | flops 262144 | bytes 1572864 | tf_op jit(solution)/shard_map/psum | solution.py:70
  358.9 0.7 dynamic-slice_convert_fusion
  359.6 20.7 %all-gather.6.cloned.1.call-done = bf16[1024,512]{1,0:T(8,128)(2,1)} async-done(((bf16[128,512]{1,0:T(8,128)(2,1)}), bf16[1024,512]{1,0:T(8,128)(2,1)}) %all-gather.6.cloned.1.call-update) | async-done | bytes 1048592 | tf_op jit(solution)/shard_map/all_gather | solution.py:73
  380.3 1.7 reshape.30
  382.0 1.3 convolution_convert_fusion.1
  383.3 1.5 copy.19
  384.9 2.8 fusion.18
  387.6 3.9 copy.14
  (17 shorter events, 0.1 us)
Async XLA Ops:
  6.5 1.6 copy-start
  6.5 245.4 %all-gather.4.cloned.1.call-start = ((), (), s32[]{:S(2)}) async-start(), calls=%async_computation.1 | async-start | bytes 1310720 | tf_op jit(solution)/shard_map/all_gather | solution.py:50
  216.2 164.1 %all-gather.6.cloned.1.call-start = ((), (), s32[]{:S(2)}) async-start(), calls=%async_computation.2 | async-start | bytes 1179648 | tf_op jit(solution)/shard_map/all_gather | solution.py:73
  251.9 15.1 %copy-start.2 = (f32[2048,1024]{1,0:T(8,128)S(1)}, f32[2048,1024]{1,0:T(8,128)}, u32[]{:S(2)}) copy-start(f32[2048,1024]{1,0:T(8,128)} %get-tuple-element.5) | copy-start | bytes 25165828
  251.9 15.1 %copy-start.4 = (bf16[1,1,128,2048]{3,2,1,0:T(8,128)(2,1)S(1)}, bf16[1,1,128,2048]{3,2,1,0:T(8,128)(2,1)}, u32[]{:S(2)}) copy-start(bf16[1,1,128,2048]{3,2,1,0:T(8,128)(2,1)} %param.8) | copy-start | bytes 1572868
  358.9 25.9 %copy-start.3 = (bf16[16,2,128,128]{3,2,1,0:T(8,128)(2,1)S(1)}, bf16[16,2,128,128]{3,2,1,0:T(8,128)(2,1)}, u32[]{:S(2)}) copy-start(bf16[16,2,128,128]{3,2,1,0:T(8,128)(2,1)} %param.6) | copy-start | bytes 3145732
  383.3 8.2 %copy-start.1 = (bf16[16,128,512]{2,1,0:T(8,128)(2,1)S(1)}, bf16[16,128,512]{2,1,0:T(8,128)(2,1)}, u32[]{:S(2)}) copy-start(bf16[16,128,512]{2,1,0:T(8,128)(2,1)} %param.5) | copy-start | bytes 6291460
Sparse Core Ops, SparseCore 0:
  216.3 25.1 all-gather.3
  359.7 20.5 all-gather.5
where the time goes:
time: 404 us; the launch traced here: 399 us
  blocking collectives  232 us (57%)
  matrix products  74.6 us (18%)
  other arithmetic  44.7 us (11%)
  waiting for transfers between devices  20.7 us (5%)
  between operations  14.5 us (4%)
  local copies, waits for them, and re-layouts  11.7 us (3%)
    all_to_all x1, blocking collectives, shards(): lax.all_to_all(outgoing, 'rows', split_axis=0, concat_axis=0, tiled=True)  191 us
    psum x1, blocking collectives, shards(): summed = lax.psum(term, 'dist')  41.1 us
    dot_general x2, matrix products, synthesize(): lax.dot_general(coeffs * weight, table, (((1,), (1,)), ((), ())), precisi...  39.7 us
    cos x1, other arithmetic, spectral_table(): return jnp.concatenate([jnp.cos(turns), jnp.sin(turns)], axis=1)  34.4 us
    all_gather x1, waiting for transfers between devices, shards(): piece = lax.all_gather(image_gradient[None], 'rows', axis=0, tiled=True)  20.7 us
    dot_general x1, matrix products, shards(): jnp.dot(lax.all_gather(projection, 'dist', axis=1, tiled=True), table, pr...  15.1 us
    dot_general x1, matrix products, shards(): jnp.dot(residual, table, precision=lax.Precision.HIGHEST, preferred_eleme...  11 us
    reduce_sum x1, other arithmetic, shards(): jnp.sum(arrived.astype(jnp.float32), axis=1).astype(jnp.bfloat16)  9.19 us
  transfers between devices with their start and end apart: 2, of which 1 were waited for; matrix products, arithmetic and copies ran while one was open for 9% of the time, Pallas kernels for 0%

commit v1 on v0

--- a/solution.py
+++ b/solution.py
@@ -70,7 +70,27 @@
     summed = lax.psum(term, "dist")
     own_cols = lax.dynamic_slice_in_dim(summed, lax.axis_index("dist") * quarter, quarter, 1)
     image_gradient = own_cols.astype(jnp.bfloat16)
-    piece = lax.all_gather(image_gradient[None], "rows", axis=0, tiled=True)
+    ways, here, step = (
+        lax.axis_size("rows"),
+        lax.axis_index("rows"),
+        image_gradient[None].shape[0],
+    )
+    shape = [n * ways if d == 0 else n for d, n in enumerate(image_gradient[None].shape)]
+    full = lax.dynamic_update_slice_in_dim(
+        jnp.zeros(shape, image_gradient[None].dtype), image_gradient[None], here * step, axis=0
+    )
+    going_up = going_down = image_gradient[None]
+    for far in range(1, ways // 2 + 1):
+        going_up = lax.ppermute(going_up, "rows", [(d, (d + 1) % ways) for d in range(ways)])
+        full = lax.dynamic_update_slice_in_dim(full, going_up, (here - far) % ways * step, axis=0)
+        if 2 * far < ways:
+            going_down = lax.ppermute(
+                going_down, "rows", [(d, (d - 1) % ways) for d in range(ways)]
+            )
+            full = lax.dynamic_update_slice_in_dim(
+                full, going_down, (here + far) % ways * step, axis=0
+            )
+    piece = full
     count = piece.shape[0]
     pick = (flat[:, None] == lax.broadcasted_iota(jnp.int32, (items, count), 1)).astype(
         jnp.bfloat16

time: 404 us -> 408 us (level)
  starting transfers between devices: 0.63 us -> 11 us
  waiting for transfers between devices: 20.7 us -> 15.4 us
    all_gather x1 -> x0, waiting for transfers between devices: 20.7 us -> none  [shards(): piece = lax.all_gather(image_gradient[None], 'rows', axis=0, tiled=True)]
    ppermute x0 -> x7, waiting for transfers between devices: none -> 15.4 us  [the longest x4 15.4 us: shards(): lax.ppermute(going_up, 'rows', [(d, (d + 1) % ways) for d in range(ways)])]
    ppermute x0 -> x7, starting transfers between devices: none -> 11 us  [the longest x3 10.6 us: shards(): lax.ppermute(going_down, 'rows', [(d, (d - 1) % ways) for d in range(ways)])]
  transfers between devices with their start and end apart: 2 -> 8, of which waited for: 1 -> 4; matrix products, arithmetic and copies ran while one was open for 9% -> 9% of each run, Pallas kernels for 0% -> 0%
where the time goes in v1:
time: 408 us; the launch traced here: 403 us
  blocking collectives  232 us (57%)
  matrix products  74.7 us (18%)
  other arithmetic  44.8 us (11%)
  waiting for transfers between devices  15.4 us (4%)
  between operations  14.8 us (4%)
  starting transfers between devices  11 us (3%)
  local copies, waits for them, and re-layouts  10.1 us (2%)
    all_to_all x1, blocking collectives, shards(): lax.all_to_all(outgoing, 'rows', split_axis=0, concat_axis=0, tiled=True)  191 us
    psum x1, blocking collectives, shards(): summed = lax.psum(term, 'dist')  40.8 us
    dot_general x2, matrix products, synthesize(): lax.dot_general(coeffs * weight, table, (((1,), (1,)), ((), ())), precisi...  39.8 us
    cos x1, other arithmetic, spectral_table(): return jnp.concatenate([jnp.cos(turns), jnp.sin(turns)], axis=1)  34.6 us
    ppermute x4, waiting for transfers between devices, shards(): lax.ppermute(going_up, 'rows', [(d, (d + 1) % ways) for d in range(ways)])  15.4 us
    dot_general x1, matrix products, shards(): jnp.dot(lax.all_gather(projection, 'dist', axis=1, tiled=True), table, pr...  15.1 us
    dot_general x1, matrix products, shards(): jnp.dot(residual, table, precision=lax.Precision.HIGHEST, preferred_eleme...  11 us
    ppermute x3, starting transfers between devices, shards(): lax.ppermute(going_down, 'rows', [(d, (d - 1) % ways) for d in range(ways)])  10.6 us
  transfers between devices with their start and end apart: 8, of which 4 were waited for; matrix products, arithmetic and copies ran while one was open for 9% of the time, Pallas kernels for 0%

profile of v1, /device:TPU:0, one launch (start us, length us, event | category | flops | bytes accessed | tf_op | source)
XLA Modules:
  0.0 402.6 jit_solution(13090835304808231746)
XLA Ops:
  6.5 0.9 copy.12
  8.1 2.5 convolution_convert_fusion.2
  10.6 2.4 copy.18
  13.0 2.3 convolution_convert_fusion
  15.3 191.0 %all_to_all.5 = bf16[8,8,128,512]{3,1,2,0:T(8,128)(2,1)} all-to-all(bf16[8,8,128,512]{3,1,2,0:T(8,128)(2,1)S(1)} %bitcast.37), channel_id=1, replica_groups=mesh['dist'=4,'rows'=8] {'rows'}, dimensions={0} | all-to-all | bytes 16777216 | tf_op jit(solution)/shard_map/all_to_all | solution.py:44
  206.3 9.2 %reduce_sum.31 = bf16[8,128,512]{2,1,0:T(8,128)(2,1)S(1)} reduce(bf16[8,8,128,512]{3,1,2,0:T(8,128)(2,1)} %all_to_all.5, bf16[]{:T(256)} %constant.78.clone.1), dimensions={1}, to_apply=%region_1.0 | reduce | flops 3670016 | bytes 9437186 | tf_op jit(solution)/shard_map/reduce_sum | solution.py:45
  215.5 0.8 convert_reduce_fusion
  217.1 34.6 %fusion.11 = (f32[2048,1024]{1,0:T(8,128)}, f32[2048,1024]{1,0:T(8,128)}) fusion(s32[1024]{0:T(1024)S(1)} %iota_add_fusion), kind=kLoop, calls=%fused_computation.18 | loop fusion | flops 29360128 | bytes 16781312 | tf_op jit(solution)/shard_map/cos | solution.py:13
  251.7 15.1 %fusion.12 = f32[128,2048]{1,0:T(8,128)S(1)} fusion(f32[128,2048]{1,0:T(8,128)} %all-gather.2.cloned.1.call-done, f32[2048,1024]{1,0:T(8,128)} %get-tuple-element.8, f32[2048,1024]{1,0:T(8,128)} %get-tuple-element.7, f32[2048]{0:T(1024)S(1)} %pad_maximum_fusion.15), kind=kOutput, calls=%fused_computation.20 | convolution fusion | flops 6446907392 | bytes 18882560 | tf_op jit(solution)/shard_map/dot_general | solution.py:49
  266.9 19.9 %fusion.16 = f32[128,2048]{1,0:T(8,128)S(1)} fusion(f32[128,2048]{1,0:T(8,128)S(1)} %fusion.12, f32[2048,1024]{1,0:T(8,128)} %get-tuple-element.8, f32[2048,1024]{1,0:T(8,128)S(1)} %copy-done.2, bf16[1,1,128,2048]{3,2,1,0:T(8,128)(2,1)S(1)} %copy-done.4), kind=kOutput, calls=%fused_computation.24 | convolution fusion | flops 6447431680 | bytes 19398656 | tf_op jit(solution)/shard_map/dot_general | solution.py:57
  286.8 11.0 %fusion.14 = f32[128,2048]{1,0:T(8,128)S(1)} fusion(f32[128,2048]{1,0:T(8,128)S(1)} %fusion.16, f32[2048,1024]{1,0:T(8,128)} %get-tuple-element.8, f32[2048,1024]{1,0:T(8,128)S(1)} %copy-done.2, f32[2048]{0:T(1024)S(1)} %pad_maximum_fusion.15), kind=kOutput, calls=%fused_computation.22 | convolution fusion | flops 6446907392 | bytes 18882560 | tf_op jit(solution)/shard_map/dot_general | solution.py:66
  297.8 19.9 %fusion.15 = f32[128,2048]{1,0:T(8,128)S(1)} fusion(f32[128,2048]{1,0:T(8,128)S(1)} %fusion.14, f32[2048,1024]{1,0:T(8,128)} %get-tuple-element.8, f32[2048,1024]{1,0:T(8,128)S(1)} %copy-done.2), kind=kOutput, calls=%fused_computation.23 | convolution fusion | flops 6446907392 | bytes 18874368 | tf_op jit(solution)/shard_map/dot_general | solution.py:57
  317.7 40.8 %all-reduce.1 = bf16[128,2048]{1,0:T(8,128)(2,1)S(1)} all-reduce(f32[128,2048]{1,0:T(8,128)S(1)} %fusion.15), channel_id=1, replica_groups=mesh['dist'=4,'rows'=8] {'dist'}, use_global_device_ids=true, to_apply=%region_3.4 | all-reduce | flops 262144 | bytes 1572864 | tf_op jit(solution)/shard_map/psum | solution.py:70
  358.7 3.5 collective-permute-start.1
  362.2 3.9 collective-permute-done
  366.1 3.5 collective-permute-start.3
  369.7 2.8 collective-permute-done.2
  372.5 3.5 collective-permute-start.5
  376.1 2.6 collective-permute-done.4
  379.0 6.1 %collective-permute-done.6 = bf16[1,128,512]{2,1,0:T(8,128)(2,1)S(1)} collective-permute-done((bf16[1,128,512]{2,1,0:T(8,128)(2,1)S(1)}, bf16[1,128,512]{2,1,0:T(8,128)(2,1)S(1)}, u32[]{:S(2)}, u32[]{:S(2)}) %collective-permute-start.6) | collective-permute-done | bytes 131104 | tf_op jit(solution)/shard_map/ppermute | solution.py:84
  385.7 1.3 convolution_convert_fusion.1
  387.0 1.5 copy.20
  388.6 2.7 fusion.18
  391.3 3.9 copy.14
  (36 shorter events, 1.9 us)
Async XLA Ops:
  6.5 1.6 copy-start
  6.5 245.2 %all-gather.2.cloned.1.call-start = ((), (), s32[]{:S(2)}) async-start(), calls=%async_computation.1 | async-start | bytes 1310720 | tf_op jit(solution)/shard_map/all_gather | solution.py:50
  251.7 15.1 %copy-start.2 = (f32[2048,1024]{1,0:T(8,128)S(1)}, f32[2048,1024]{1,0:T(8,128)}, u32[]{:S(2)}) copy-start(f32[2048,1024]{1,0:T(8,128)} %get-tuple-element.7) | copy-start | bytes 25165828
  251.7 15.1 %copy-start.4 = (bf16[1,1,128,2048]{3,2,1,0:T(8,128)(2,1)S(1)}, bf16[1,1,128,2048]{3,2,1,0:T(8,128)(2,1)}, u32[]{:S(2)}) copy-start(bf16[1,1,128,2048]{3,2,1,0:T(8,128)(2,1)} %param.8) | copy-start | bytes 1572868
  358.6 7.5 %collective-permute-start = (bf16[1,128,512]{2,1,0:T(8,128)(2,1)S(1)}, bf16[1,128,512]{2,1,0:T(8,128)(2,1)S(1)}, u32[]{:S(2)}, u32[]{:S(2)}) collective-permute-start(bf16[1,128,512]{2,1,0:T(8,128)(2,1)S(1)} %get-tuple-element.6), channel_id=1, source_target_pairs={{0,1},{1,2},{2,3},{3,4},{4,5},{5,6},{6,7},{7,0},{8,9},{9,10},{10,1... | collective-permute-start | bytes 393224 | tf_op jit(solution)/shard_map/ppermute | solution.py:84
  358.7 7.5 %collective-permute-start.1 = (bf16[1,128,512]{2,1,0:T(8,128)(2,1)S(1)}, bf16[1,128,512]{2,1,0:T(8,128)(2,1)S(1)}, u32[]{:S(2)}, u32[]{:S(2)}) collective-permute-start(bf16[1,128,512]{2,1,0:T(8,128)(2,1)S(1)} %get-tuple-element.6), channel_id=1, source_target_pairs={{0,7},{1,0},{2,1},{3,2},{4,3},{5,4},{6,5},{7,6},{8,15},{9,8},{10,9... | collective-permute-start | bytes 393224 | tf_op jit(solution)/shard_map/ppermute | solution.py:87
  366.1 6.3 %collective-permute-start.2 = (bf16[1,128,512]{2,1,0:T(8,128)(2,1)S(1)}, bf16[1,128,512]{2,1,0:T(8,128)(2,1)S(1)}, u32[]{:S(2)}, u32[]{:S(2)}) collective-permute-start(bf16[1,128,512]{2,1,0:T(8,128)(2,1)S(1)} %collective-permute-done), channel_id=1, source_target_pairs={{0,1},{1,2},{2,3},{3,4},{4,5},{5,6},{6,7},{7,0},{8,9},{9,10},{10,1... | collective-permute-start | bytes 393224 | tf_op jit(solution)/shard_map/ppermute | solution.py:84
  366.1 6.3 %collective-permute-start.3 = (bf16[1,128,512]{2,1,0:T(8,128)(2,1)S(1)}, bf16[1,128,512]{2,1,0:T(8,128)(2,1)S(1)}, u32[]{:S(2)}, u32[]{:S(2)}) collective-permute-start(bf16[1,128,512]{2,1,0:T(8,128)(2,1)S(1)} %collective-permute-done.1), channel_id=1, source_target_pairs={{0,7},{1,0},{2,1},{3,2},{4,3},{5,4},{6,5},{7,6},{8,15},{9,8},{10,9... | collective-permute-start | bytes 393224 | tf_op jit(solution)/shard_map/ppermute | solution.py:87
  372.5 6.2 %collective-permute-start.4 = (bf16[1,128,512]{2,1,0:T(8,128)(2,1)S(1)}, bf16[1,128,512]{2,1,0:T(8,128)(2,1)S(1)}, u32[]{:S(2)}, u32[]{:S(2)}) collective-permute-start(bf16[1,128,512]{2,1,0:T(8,128)(2,1)S(1)} %collective-permute-done.2), channel_id=1, source_target_pairs={{0,1},{1,2},{2,3},{3,4},{4,5},{5,6},{6,7},{7,0},{8,9},{9,10},{10,1... | collective-permute-start | bytes 393224 | tf_op jit(solution)/shard_map/ppermute | solution.py:84
  372.5 6.5 %collective-permute-start.5 = (bf16[1,128,512]{2,1,0:T(8,128)(2,1)S(1)}, bf16[1,128,512]{2,1,0:T(8,128)(2,1)S(1)}, u32[]{:S(2)}, u32[]{:S(2)}) collective-permute-start(bf16[1,128,512]{2,1,0:T(8,128)(2,1)S(1)} %collective-permute-done.3), channel_id=1, source_target_pairs={{0,7},{1,0},{2,1},{3,2},{4,3},{5,4},{6,5},{7,6},{8,15},{9,8},{10,9... | collective-permute-start | bytes 393224 | tf_op jit(solution)/shard_map/ppermute | solution.py:87
  376.0 12.5 %copy-start.3 = (bf16[16,2,128,128]{3,2,1,0:T(8,128)(2,1)S(1)}, bf16[16,2,128,128]{3,2,1,0:T(8,128)(2,1)}, u32[]{:S(2)}) copy-start(bf16[16,2,128,128]{3,2,1,0:T(8,128)(2,1)} %param.6) | copy-start | bytes 3145732
  378.7 6.5 %collective-permute-start.6 = (bf16[1,128,512]{2,1,0:T(8,128)(2,1)S(1)}, bf16[1,128,512]{2,1,0:T(8,128)(2,1)S(1)}, u32[]{:S(2)}, u32[]{:S(2)}) collective-permute-start(bf16[1,128,512]{2,1,0:T(8,128)(2,1)S(1)} %collective-permute-done.4), channel_id=1, source_target_pairs={{0,1},{1,2},{2,3},{3,4},{4,5},{5,6},{6,7},{7,0},{8,9},{9,10},{10,1... | collective-permute-start | bytes 393224 | tf_op jit(solution)/shard_map/ppermute | solution.py:84
  387.0 8.2 %copy-start.1 = (bf16[16,128,512]{2,1,0:T(8,128)(2,1)S(1)}, bf16[16,128,512]{2,1,0:T(8,128)(2,1)}, u32[]{:S(2)}) copy-start(bf16[16,128,512]{2,1,0:T(8,128)(2,1)} %param.5) | copy-start | bytes 6291460
Sparse Core Ops, SparseCore 0:
  216.5 25.1 all-gather.1
